TPU v7x, 32 devices: a whole 2x2x4 slice. The times are simulated.
32 devices in a mesh: pts: 32 (over z, y, x, core).
Axes of the slice: x: 2, y: 2, z: 4, core: 2. Of those that a mesh axis runs over, the one named last changes fastest.
Arguments:
- features: float32 [65536, 128], P('pts'), may hold values from -6 to 6
- factor: float32 [65536, 1024], P('pts'), may hold values from -0.375 to 0.375
- targets: float32 [65536, 256], P('pts'), may hold values from -6 to 6
- pivots: int32 [4, 256], replicated, may hold values from 0 to 65535, as said below
Outputs:
- residuals: float32 [65536, 256], P('pts')
- scores: float32 [4, 256, 256], replicated
Inputs may be any that keep to these rules, and one draw needn't show every extreme that they name: Owners of pivots are uneven: low point indices are picked more often. Indices may repeat.
All inputs are finite; a program needn't handle non-finite values.
Results may differ from a plain program's by a relative error of at most 0.0003.
Values sent between devices are 32-bit elements; how exact they have to be, the bound alone decides.
A program may use at most 192 MiB of HBM per device.

v0:
```python
import jax
import jax.numpy as jnp
from jax import lax
from jax.sharding import PartitionSpec as P

FEATS = 128
PIV = 256
BLOCKS = 4


def hdot(a, b):
    return jnp.dot(a, b, precision=lax.Precision.HIGHEST, preferred_element_type=jnp.float32)


def kernel_cols(points, pivot_feats):
    left = jnp.sum(points * points, axis=1)[:, None]
    right = jnp.sum(pivot_feats * pivot_feats, axis=1)[None, :]
    cross = hdot(points, pivot_feats.T)
    return jnp.exp(-(left + right - 2.0 * cross) * (0.5 / FEATS))


def owned_rows(table, index_list, offset, count):
    local = index_list - offset
    owned = (local >= 0) & (local < count)
    safe = jnp.clip(local, 0, count - 1)
    return jnp.take(table, safe, axis=0) * owned[:, None].astype(table.dtype)


def per_device(features, factor, targets, pivots):
    count = features.shape[0]
    npts = count * lax.axis_size("pts")
    offset = lax.axis_index("pts") * count
    eye = jnp.eye(PIV, dtype=jnp.float32)
    resid = targets
    extras = []
    score_list = []
    for block in range(BLOCKS):
        idx = pivots[block]
        if block > 0:
            joined = jnp.concatenate(extras, axis=1)
        if block > 0:
            extra_part = owned_rows(joined, idx, offset, count)
        else:
            extra_part = jnp.zeros((PIV, 8), jnp.float32)
        piv_feats, piv_rows, piv_extra = lax.psum(
            (
                owned_rows(features, idx, offset, count),
                owned_rows(factor, idx, offset, count),
                extra_part,
            ),
            "pts",
        )
        cols = kernel_cols(features, piv_feats) - hdot(factor, piv_rows.T)
        if block > 0:
            cols = cols - hdot(joined, piv_extra.T)
        gram = lax.psum(hdot(cols.T, cols), "pts")
        lower = jnp.linalg.cholesky(gram / npts + 0.05 * eye)
        normed = lax.linalg.triangular_solve(
            lower, cols, left_side=False, lower=True, transpose_a=True
        )
        qq, qy = lax.psum((hdot(normed.T, normed), hdot(normed.T, resid)), "pts")
        scaled_qq = qq / npts
        ridge = jnp.linalg.cholesky(scaled_qq + 0.1 * eye)
        middle = lax.linalg.triangular_solve(ridge, qy / npts, left_side=True, lower=True)
        beta = lax.linalg.triangular_solve(
            ridge, middle, left_side=True, lower=True, transpose_a=True
        )
        resid = resid - hdot(normed, beta)
        score_list.append(qy / jnp.sqrt(jnp.float32(npts)))
        extras.append(normed * (1.0 / jnp.sqrt(jnp.float32(PIV))))
    return (resid, jnp.stack(score_list))


def solution(mesh):
    in_specs = (P("pts", None), P("pts", None), P("pts", None), P())
    out_specs = (P("pts", None), P())
    return jax.shard_map(
        per_device, mesh=mesh, in_specs=in_specs, out_specs=out_specs, check_vma=False
    )
```

profile of v0, /device:TPU:0, one launch (start us, length us, event | category | flops | bytes accessed | tf_op | source)
XLA Modules:
  0.0 1928.5 jit_solution(473149198986484992)
XLA Ops:
  26.0 126.0 %all-reduce.34.cloned.1.call-done = (f32[256,1024]{1,0:T(8,128)}, f32[256,128]{1,0:T(8,128)}) async-done(((f32[256,1024]{1,0:T(8,128)}, f32[256,128]{1,0:T(8,128)}), (f32[256,1024]{1,0:T(8,128)}, f32[256,128]{1,0:T(8,128)})) %all-reduce.34.cloned.1.call-update) | async-done | bytes 1179664 | tf_op jit(solution)/shard_map/psum | solution.py:45
  169.3 122.7 %all-reduce.18.cloned.1.call-done = f32[256,256]{0,1:T(8,128)} async-done(((f32[256,256]{0,1:T(8,128)}), f32[256,256]{0,1:T(8,128)}) %all-reduce.18.cloned.1.call-update) | async-done | bytes 262160 | tf_op jit(solution)/shard_map/psum | solution.py:56
  321.4 11.7 cholesky.399
  345.2 20.5 %custom-call.34 = f32[2,128,128]{1,2,0:T(8,128)S(1)} custom-call(f32[2,128,128]{2,1,0:T(8,128)} %copy-done.72), custom_call_target="InvertDiagBlocksLowerTriangular" | custom-call | tf_op jit(solution)/shard_map/triangular_solve/custom-call.0 | solution.py:58
  385.7 121.8 %all-reduce.32.cloned.1.call-done = (f32[256,1024]{1,0:T(8,128)}, f32[256,128]{1,0:T(8,128)}, f32[256,256]{1,0:T(8,128)}) async-done(((f32[256,1024]{1,0:T(8,128)}, f32[256,128]{1,0:T(8,128)}, f32[256,256]{1,0:T(8,128)}), (f32[256,1024]{1,0:T(8,128)}, f32[256,128]{1,0:T(8,128)}, f32[256,256]{1,0:T(8,128)})) %all-reduce.32.cloned.1.call-update) | async-done | bytes 1441808 | tf_op jit(solution)/shard_map/psum | solution.py:45
  527.7 122.5 %all-reduce.20.cloned.1.call-done = f32[256,256]{0,1:T(8,128)} async-done(((f32[256,256]{0,1:T(8,128)}), f32[256,256]{0,1:T(8,128)}) %all-reduce.20.cloned.1.call-update) | async-done | bytes 262160 | tf_op jit(solution)/shard_map/psum | solution.py:56
  679.0 11.7 cholesky.467
  701.8 20.5 %custom-call.39 = f32[2,128,128]{1,2,0:T(8,128)S(1)} custom-call(f32[2,128,128]{2,1,0:T(8,128)} %copy-done.73), custom_call_target="InvertDiagBlocksLowerTriangular" | custom-call | tf_op jit(solution)/shard_map/triangular_solve/custom-call.0 | solution.py:58
  762.3 113.8 %all-reduce.30.cloned.1.call-done = (f32[256,1024]{1,0:T(8,128)}, f32[256,128]{1,0:T(8,128)}, f32[256,512]{1,0:T(8,128)}) async-done(((f32[256,1024]{1,0:T(8,128)}, f32[256,128]{1,0:T(8,128)}, f32[256,512]{1,0:T(8,128)}), (f32[256,1024]{1,0:T(8,128)}, f32[256,128]{1,0:T(8,128)}, f32[256,512]{1,0:T(8,128)})) %all-reduce.30.cloned.1.call-update) | async-done | bytes 1703952 | tf_op jit(solution)/shard_map/psum | solution.py:45
  901.9 123.9 %all-reduce.28.cloned.1.call-done = (f32[256,256]{0,1:T(8,128)}, f32[256,256]{0,1:T(8,128)}, f32[256,256]{0,1:T(8,128)}) async-done(((f32[256,256]{0,1:T(8,128)}, f32[256,256]{0,1:T(8,128)}, f32[256,256]{0,1:T(8,128)}), (f32[256,256]{0,1:T(8,128)}, f32[256,256]{0,1:T(8,128)}, f32[256,256]{0,1:T(8,128)})) %all-reduce.28.cloned.1.call-update) | async-done | bytes 786448 | tf_op jit(solution)/shard_map/psum | solution.py:61
  1054.7 12.1 cholesky.535
  1076.9 20.5 %custom-call.44 = f32[2,128,128]{1,2,0:T(8,128)S(1)} custom-call(f32[2,128,128]{2,1,0:T(8,128)} %copy-done.74), custom_call_target="InvertDiagBlocksLowerTriangular" | custom-call | tf_op jit(solution)/shard_map/triangular_solve/custom-call.0 | solution.py:58
  1149.5 11.7 cholesky.433
  1169.5 20.9 %custom-call.37 = f32[2,128,128]{1,2,0:T(8,128)S(1)} custom-call(f32[2,128,128]{2,1,0:T(8,128)} %copy-done.75), custom_call_target="InvertDiagBlocksLowerTriangular" | custom-call | tf_op jit(solution)/shard_map/triangular_solve/custom-call.5 | solution.py:65
  1210.0 131.8 %all-reduce.26.cloned.1.call-done = (f32[256,256]{0,1:T(8,128)}, f32[256,256]{0,1:T(8,128)}, f32[256,1024]{1,0:T(8,128)}, f32[256,128]{1,0:T(8,128)}, f32[256,768]{1,0:T(8,128)}) async-done(((f32[256,256]{0,1:T(8,128)}, f32[256,256]{0,1:T(8,128)}, f32[256,1024]{1,0:T(8,128)}, f32[256,128]{1,0:T(8,128)}, f32[256,768]{1,0:T(8,128)}), (f32[256,256]{0,1:T(8,128)}, f32[256,256]{0,1:T(8,128)}, ...) | async-done | bytes 2490384 | tf_op jit(solution)/shard_map/psum | solution.py:61
  1363.1 11.9 cholesky.484
  1403.8 20.1 %custom-call.42 = f32[2,128,128]{1,2,0:T(8,128)S(1)} custom-call(f32[2,128,128]{2,1,0:T(8,128)S(1)} %get-tuple-element.91), custom_call_target="InvertDiagBlocksLowerTriangular" | custom-call | tf_op jit(solution)/shard_map/triangular_solve/custom-call.5 | solution.py:65
  1437.6 128.9 %all-reduce.24.cloned.1.call-done = (f32[256,256]{0,1:T(8,128)}, f32[256,256]{0,1:T(8,128)}, f32[256,256]{0,1:T(8,128)}) async-done(((f32[256,256]{0,1:T(8,128)}, f32[256,256]{0,1:T(8,128)}, f32[256,256]{0,1:T(8,128)}), (f32[256,256]{0,1:T(8,128)}, f32[256,256]{0,1:T(8,128)}, f32[256,256]{0,1:T(8,128)})) %all-reduce.24.cloned.1.call-update) | async-done | bytes 786448 | tf_op jit(solution)/shard_map/psum | solution.py:61
  1614.9 20.9 %custom-call.49 = f32[2,128,128]{1,2,0:T(8,128)S(1)} custom-call(f32[2,128,128]{2,1,0:T(8,128)} %copy-done.76), custom_call_target="InvertDiagBlocksLowerTriangular" | custom-call | tf_op jit(solution)/shard_map/triangular_solve/custom-call.0 | solution.py:58
  1662.4 11.9 cholesky.569
  1682.1 20.5 %custom-call.47 = f32[2,128,128]{1,2,0:T(8,128)S(1)} custom-call(f32[2,128,128]{2,1,0:T(8,128)} %copy-done.77), custom_call_target="InvertDiagBlocksLowerTriangular" | custom-call | tf_op jit(solution)/shard_map/triangular_solve/custom-call.5 | solution.py:65
  1716.8 127.3 %all-reduce.22.cloned.1.call-done = (f32[256,256]{0,1:T(8,128)}, f32[256,256]{0,1:T(8,128)}) async-done(((f32[256,256]{0,1:T(8,128)}, f32[256,256]{0,1:T(8,128)}), (f32[256,256]{0,1:T(8,128)}, f32[256,256]{0,1:T(8,128)})) %all-reduce.22.cloned.1.call-update) | async-done | bytes 524304 | tf_op jit(solution)/shard_map/psum | solution.py:61
  1847.5 11.9 cholesky.620
  1891.1 20.7 %custom-call.52 = f32[2,128,128]{1,2,0:T(8,128)S(1)} custom-call(f32[2,128,128]{2,1,0:T(8,128)} %copy-done.71), custom_call_target="InvertDiagBlocksLowerTriangular" | custom-call | tf_op jit(solution)/shard_map/triangular_solve/custom-call.5 | solution.py:65
  (497 shorter events, 572.0 us)
Async XLA Ops:
  7.2 144.9 %all-reduce.34.cloned.1.call-start = ((), (), s32[]{:S(2)}) async-start(), calls=%async_computation.8 | async-start | bytes 2359296 | tf_op jit(solution)/shard_map/psum | solution.py:45
  9.3 15.5 copy-start.83
  10.2 14.7 copy-start.78
  18.0 274.0 %all-reduce.18.cloned.1.call-start = ((), (), s32[]{:S(2)}) async-start(), calls=%async_computation | async-start | bytes 524288 | tf_op jit(solution)/shard_map/psum | solution.py:56
  167.9 339.6 %all-reduce.32.cloned.1.call-start = ((), (), s32[]{:S(2)}) async-start(), calls=%async_computation.7 | async-start | bytes 2883584 | tf_op jit(solution)/shard_map/psum | solution.py:45
  375.4 274.7 %all-reduce.20.cloned.1.call-start = ((), (), s32[]{:S(2)}) async-start(), calls=%async_computation.1 | async-start | bytes 524288 | tf_op jit(solution)/shard_map/psum | solution.py:56
  383.3 143.0 %copy-start.85 = (pred[256]{0:T(512)(128)(4,1)}, pred[256]{0:T(512)(128)(4,1)S(1)}, u32[]{:S(2)}) copy-start(pred[256]{0:T(512)(128)(4,1)S(1)} %get-tuple-element.278) | copy-start | bytes 772
  526.0 350.1 %all-reduce.30.cloned.1.call-start = ((), (), s32[]{:S(2)}) async-start(), calls=%async_computation.6 | async-start | bytes 3407872 | tf_op jit(solution)/shard_map/psum | solution.py:45
  743.5 282.3 %all-reduce.28.cloned.1.call-start = ((), (), s32[]{:S(2)}) async-start(), calls=%async_computation.5 | async-start | bytes 1572864 | tf_op jit(solution)/shard_map/psum | solution.py:61
  896.5 445.2 %all-reduce.26.cloned.1.call-start = ((), (), s32[]{:S(2)}) async-start(), calls=%async_computation.4 | async-start | bytes 4980736 | tf_op jit(solution)/shard_map/psum | solution.py:61
  1121.5 43.4 %copy-start.90 = (s32[2,2]{1,0:T(2,128)S(1)}, s32[2,2]{1,0:T(2,128)}, u32[]{:S(2)}) copy-start(s32[2,2]{1,0:T(2,128)} %get-tuple-element.749) | copy-start | bytes 52
  1205.2 361.4 %all-reduce.24.cloned.1.call-start = ((), (), s32[]{:S(2)}) async-start(), calls=%async_computation.3 | async-start | bytes 1572864 | tf_op jit(solution)/shard_map/psum | solution.py:61
  1362.9 61.0 %copy-start.69 = (f32[256,256]{0,1:T(8,128)S(1)}, f32[256,256]{0,1:T(8,128)}, u32[]{:S(2)}) copy-start(f32[256,256]{0,1:T(8,128)} %get-tuple-element.171) | copy-start | bytes 786436
  1399.7 26.8 %copy-start.24 = (f32[128,2048]{1,0:T(8,128)S(1)}, f32[128,2048]{1,0:T(8,128)}, u32[]{:S(2)}) copy-start(f32[128,2048]{1,0:T(8,128)} %copy-done.21) | copy-start | bytes 3145732
  1399.7 26.8 %copy-start.41 = (f32[2048,128]{0,1:T(8,128)S(1)}, f32[2048,128]{0,1:T(8,128)}, u32[]{:S(2)}) copy-start(f32[2048,128]{0,1:T(8,128)} %copy-done.38) | copy-start | bytes 3145732
  1437.4 406.7 %all-reduce.22.cloned.1.call-start = ((), (), s32[]{:S(2)}) async-start(), calls=%async_computation.2 | async-start | bytes 1048576 | tf_op jit(solution)/shard_map/psum | solution.py:61
  1568.2 67.6 %copy-start.14 = (f32[2048,256]{0,1:T(8,128)S(1)}, f32[2048,256]{0,1:T(8,128)}, u32[]{:S(2)}) copy-start(f32[2048,256]{0,1:T(8,128)} %copy-done.13) | copy-start | bytes 6291460
  1677.1 29.2 %copy-start.26 = (f32[2048,256]{1,0:T(8,128)S(1)}, f32[2048,256]{1,0:T(8,128)}, u32[]{:S(2)}) copy-start(f32[2048,256]{1,0:T(8,128)} %copy-done.25) | copy-start | bytes 6291460
  1712.6 133.3 %copy-start.54 = (f32[1,256,256]{1,2,0:T(8,128)S(1)}, f32[1,256,256]{1,2,0:T(8,128)}, u32[]{:S(2)}) copy-start(f32[1,256,256]{1,2,0:T(8,128)} %get-tuple-element.209) | copy-start | bytes 786436
  1712.6 133.3 %copy-start.55 = (f32[1,256,256]{1,2,0:T(8,128)S(1)}, f32[1,256,256]{1,2,0:T(8,128)}, u32[]{:S(2)}) copy-start(f32[1,256,256]{1,2,0:T(8,128)} %get-tuple-element.211) | copy-start | bytes 786436
  1712.6 133.3 %copy-start.56 = (f32[1,256,256]{1,2,0:T(8,128)S(1)}, f32[1,256,256]{1,2,0:T(8,128)}, u32[]{:S(2)}) copy-start(f32[1,256,256]{1,2,0:T(8,128)} %get-tuple-element.213) | copy-start | bytes 786436
  1847.5 21.8 %copy-start.62 = (f32[256,256]{1,0:T(8,128)}, f32[256,256]{1,0:T(8,128)S(1)}, u32[]{:S(2)}) copy-start(f32[256,256]{1,0:T(8,128)S(1)} %fusion.52) | copy-start | bytes 786436
  1869.5 46.0 %copy-start.29 = (f32[2048,256]{1,0:T(8,128)S(1)}, f32[2048,256]{1,0:T(8,128)}, u32[]{:S(2)}) copy-start(f32[2048,256]{1,0:T(8,128)} %copy-done.28) | copy-start | bytes 6291460
  1869.5 46.0 %copy-start.34 = (f32[128,2048]{1,0:T(8,128)S(1)}, f32[128,2048]{1,0:T(8,128)}, u32[]{:S(2)}) copy-start(f32[128,2048]{1,0:T(8,128)} %copy-done.32) | copy-start | bytes 3145732
  (76 other events, 239.1 us)
Sparse Core Ops, SparseCore 0:
  18.1 133.8 all-reduce.33
  168.0 123.9 all-reduce.17
  375.6 131.8 all-reduce.31
  526.1 124.0 all-reduce.19
  743.7 132.3 all-reduce.29
  896.6 129.1 all-reduce.27
  1205.3 136.4 all-reduce.25
  1437.5 128.9 all-reduce.23
  1716.9 127.1 all-reduce.21
where the time goes:
time: 1940 us; the launch traced here: 1930 us
  waiting for transfers between devices  1120 us (58%)
  other arithmetic  502 us (26%)
  matrix products  164 us (8%)
  local copies, waits for them, and re-layouts  116 us (6%)
  between operations  26.5 us (1%)
    psum x4, waiting for transfers between devices, per_device(): qq, qy = lax.psum((hdot(normed.T, normed), hdot(normed.T, resid)), 'pts')  512 us
    psum x3, waiting for transfers between devices, per_device(): lax.psum((owned_rows(features, idx, offset, count), owned_rows(factor, id...  362 us
    psum x2, waiting for transfers between devices, per_device(): gram = lax.psum(hdot(cols.T, cols), 'pts')  245 us
    another operation x28, other arithmetic, per_device(): lower = jnp.linalg.cholesky(gram / npts + 0.05 * eye)  143 us
    another operation x28, other arithmetic, per_device(): ridge = jnp.linalg.cholesky(scaled_qq + 0.1 * eye)  139 us
    dot_general x27, matrix products, hdot(): jnp.dot(a, b, precision=lax.Precision.HIGHEST, preferred_element_type=jnp...  125 us
    another operation x9, other arithmetic, per_device(): lax.linalg.triangular_solve(lower, cols, left_side=False, lower=True, tra...  86.8 us
    another operation x8, other arithmetic, per_device(): lax.linalg.triangular_solve(ridge, middle, left_side=True, lower=True, tr...  84.2 us
  transfers between devices with their start and end apart: 9, of which 9 were waited for; matrix products, arithmetic and copies ran while one was open for 3% of the time, Pallas kernels for 0%

commit v1 on v0

v1 whole, which is shorter than its diff:
```python
import jax
import jax.numpy as jnp
from jax import lax
from jax.sharding import PartitionSpec as P

LOAD = 0.05
RIDGE = 0.1


def dot(a, b, precision=lax.Precision.HIGH):
    return jnp.dot(a, b, precision=precision, preferred_element_type=jnp.float32)


def dot_tn(a, b, precision=lax.Precision.HIGH):
    return lax.dot_general(
        a, b, (((0,), (0,)), ((), ())), precision=precision, preferred_element_type=jnp.float32
    )


def dot_nt(a, b, precision=lax.Precision.HIGH):
    return lax.dot_general(
        a, b, (((1,), (1,)), ((), ())), precision=precision, preferred_element_type=jnp.float32
    )


def fdot(a, b):
    return dot(a, b, lax.Precision.HIGHEST)


def fdot_tn(a, b):
    return dot_tn(a, b, lax.Precision.HIGHEST)


def fdot_nt(a, b):
    return dot_nt(a, b, lax.Precision.HIGHEST)


def raw_cols(points, rows, pivot_feats, pivot_rows):
    left = jnp.sum(points * points, axis=1)[:, None]
    right = jnp.sum(pivot_feats * pivot_feats, axis=1)[None, :]
    cross = dot_nt(points, pivot_feats)
    scale = 0.5 / points.shape[1]
    return jnp.exp(-(left + right - 2.0 * cross) * scale) - dot_nt(rows, pivot_rows)


def owned_rows(table, index_list, offset, count):
    local = index_list - offset
    owned = (local >= 0) & (local < count)
    safe = jnp.clip(local, 0, count - 1)
    return jnp.take(table, safe, axis=0) * owned[:, None].astype(table.dtype)


def ridge_inverse(inv_lower):
    eye = jnp.eye(inv_lower.shape[0], dtype=jnp.float32)
    mat = (1.0 + RIDGE) * eye - LOAD * fdot_nt(inv_lower, inv_lower)
    first = 2.0 / (1.0 + 2.0 * RIDGE)
    err = first * (1.0 + RIDGE) - 1.0
    scale = 2.0 / (2.0 - err * err)
    est = scale * first * (2.0 * eye - first * mat)
    err = scale - 1.0
    while err > 1e-8:
        scale = 2.0 / (2.0 - err * err)
        est = scale * fdot(est, 2.0 * eye - fdot(mat, est))
        err = scale - 1.0
    return est


def factor_inverse(mat):
    lower = jnp.linalg.cholesky(mat)
    eye = jnp.eye(mat.shape[0], dtype=jnp.float32)
    return lax.linalg.triangular_solve(lower, eye, left_side=True, lower=True)


def chain(grams, at_pivots, blocks, piv, npts):
    eye = jnp.eye(piv, dtype=jnp.float32)
    scores, steps = [], []
    for c in range(blocks):
        own, rest = grams[c][:, :piv], grams[c][:, piv:]
        inv_lower = factor_inverse(own / npts + LOAD * eye)
        product = fdot(inv_lower, rest[:, (blocks - 1 - c) * piv :])
        scores.append(product * (1.0 / npts**0.5))
        beta = fdot(ridge_inverse(inv_lower), product * (1.0 / npts))
        width = (blocks - 1 - c) * piv
        if width:
            seen = at_pivots[c]
            coeff = fdot_tn(inv_lower, jnp.concatenate([fdot_nt(inv_lower, seen) * (1.0 / piv), beta], 1))
            after = rest - fdot(own, coeff)
            for b in range(c + 1, blocks):
                lo = (b - c - 1) * piv
                grams[b] = (
                    grams[b]
                    - fdot_tn(rest[:, lo : lo + piv], coeff[:, lo:])
                    - fdot_tn(coeff[:, lo : lo + piv], after[:, lo:])
                )
            for d in range(c + 1, blocks - 1):
                lo = (d - c - 1) * piv
                at_pivots[d] = at_pivots[d] - fdot(seen[lo + piv :], coeff[:, lo : lo + piv])
        else:
            coeff = fdot_tn(inv_lower, beta)
        steps.append(coeff)
    weights = [None] * blocks
    for c in reversed(range(blocks)):
        own = steps[c][:, (blocks - 1 - c) * piv :]
        if c < blocks - 1:
            own = own - fdot(steps[c][:, : (blocks - 1 - c) * piv], jnp.concatenate(weights[c + 1 :], 0))
        weights[c] = own
    return jnp.concatenate(weights, 0), scores


def per_device(features, factor, targets, pivots):
    count = features.shape[0]
    blocks, piv = pivots.shape
    npts = count * lax.axis_size("pts")
    offset = lax.axis_index("pts") * count
    idx = pivots.reshape(-1)
    piv_feats, piv_rows = lax.psum(
        (owned_rows(features, idx, offset, count), owned_rows(factor, idx, offset, count)), "pts"
    )
    cols = raw_cols(features, factor, piv_feats, piv_rows)
    joined = jnp.concatenate([cols, targets], axis=1)
    grams = lax.psum(
        [dot_tn(cols[:, c * piv : (c + 1) * piv], joined[:, c * piv :]) for c in range(blocks)], "pts"
    )
    at_pivots = [
        raw_cols(
            piv_feats[(c + 1) * piv :],
            piv_rows[(c + 1) * piv :],
            piv_feats[c * piv : (c + 1) * piv],
            piv_rows[c * piv : (c + 1) * piv],
        )
        for c in range(blocks - 1)
    ]
    weights, scores = chain(list(grams), at_pivots, blocks, piv, npts)
    return targets - dot(cols, weights), jnp.stack(scores)


def solution(mesh):
    in_specs = (P("pts", None), P("pts", None), P("pts", None), P())
    out_specs = (P("pts", None), P())
    return jax.shard_map(
        per_device, mesh=mesh, in_specs=in_specs, out_specs=out_specs, check_vma=False
    )
```

time: 1940 us -> 727 us (0.37)
  waiting for transfers between devices: 1120 us -> 277 us
  other arithmetic: 502 us -> 241 us
  local copies, waits for them, and re-layouts: 116 us -> 43.9 us
  matrix products: 164 us -> 135 us
    psum x6 -> x1, waiting for transfers between devices: 757 us -> 133 us  [per_device(): lax.psum([dot_tn(cols[:, c * piv:(c + 1) * piv], joined[:, c * piv:]) for...]
    another operation x78 -> x41, other arithmetic: 460 us -> 227 us  [the longest x27 139 us: factor_inverse(): lower = jnp.linalg.cholesky(mat)]
    psum x3 -> x1, waiting for transfers between devices: 362 us -> 144 us  [per_device(): lax.psum((owned_rows(features, idx, offset, count), owned_rows(factor, id...]
    another operation x52 -> x20, matrix products: 38.9 us -> 12.4 us  [the longest x12 6.56 us: factor_inverse(): return lax.linalg.triangular_solve(lower, eye, left_side=True, lower=True)]
    gather x11 -> x2, local copies, waits for them, and re-layouts: 37 us -> 12.7 us  [owned_rows(): return jnp.take(table, safe, axis=0) * owned[:, None].astype(table.dtype)]
    dot_general x27 -> x85, matrix products: 125 us -> 123 us  [the longest x50 44.9 us: dot(): jnp.dot(a, b, precision=precision, preferred_element_type=jnp.float32)]
  transfers between devices with their start and end apart: 9 -> 2, of which waited for: 9 -> 2; matrix products, arithmetic and copies ran while one was open for 3% -> 1% of each run, Pallas kernels for 0% -> 0%
where the time goes in v1:
time: 727 us; the launch traced here: 719 us
  waiting for transfers between devices  277 us (38%)
  other arithmetic  241 us (33%)
  matrix products  135 us (19%)
  local copies, waits for them, and re-layouts  43.9 us (6%)
  between operations  20.7 us (3%)
    psum x1, waiting for transfers between devices, per_device(): lax.psum((owned_rows(features, idx, offset, count), owned_rows(factor, id...  144 us
    another operation x27, other arithmetic, factor_inverse(): lower = jnp.linalg.cholesky(mat)  139 us
    psum x1, waiting for transfers between devices, per_device(): lax.psum([dot_tn(cols[:, c * piv:(c + 1) * piv], joined[:, c * piv:]) for...  133 us
    another operation x9, other arithmetic, factor_inverse(): return lax.linalg.triangular_solve(lower, eye, left_side=True, lower=True)  83 us
    dot_general x50, matrix products, dot(): jnp.dot(a, b, precision=precision, preferred_element_type=jnp.float32)  44.9 us
    dot_general x20, matrix products, dot_tn(): lax.dot_general(a, b, (((0,), (0,)), ((), ())), precision=precision, pref...  41.4 us
    dot_general x15, matrix products, dot_nt(): lax.dot_general(a, b, (((1,), (1,)), ((), ())), precision=precision, pref...  36.6 us
    another operation x29, local copies, waits for them, and re-layouts, factor_inverse(): return lax.linalg.triangular_solve(lower, eye, left_side=True, lower=True)  17.7 us
  transfers between devices with their start and end apart: 2, of which 2 were waited for; matrix products, arithmetic and copies ran while one was open for 1% of the time, Pallas kernels for 0%

profile of v1, /device:TPU:0, one launch (start us, length us, event | category | flops | bytes accessed | tf_op | source)
XLA Modules:
  0.0 718.5 jit_solution(2887558791544863350)
XLA Ops:
  8.7 9.9 %gather_fusion.1 = f32[1024,1024]{1,0:T(8,128)} fusion(f32[2048,1024]{1,0:T(8,128)} %param.8, s32[1024]{0:T(1024)S(1)} %broadcast_clamp_fusion), kind=kCustom, calls=%fused_computation.1 | custom fusion | bytes 8392704 | tf_op jit(solution)/shard_map/jit(_take)/gather | solution.py:50
  30.4 144.2 %all-reduce.8.cloned.1.call-done = (f32[1024,128]{1,0:T(8,128)}, f32[1024,1024]{1,0:T(8,128)}) async-done(((f32[1024,128]{1,0:T(8,128)}, f32[1024,1024]{1,0:T(8,128)}), (f32[1024,128]{1,0:T(8,128)}, f32[1024,1024]{1,0:T(8,128)})) %all-reduce.8.cloned.1.call-update) | async-done | bytes 4718608 | tf_op jit(solution)/shard_map/psum | solution.py:116
  174.5 4.7 fusion.276
  179.5 18.4 %bitcast_subtract_fusion = f32[2048,1024]{0,1:T(8,128)} fusion(f32[1024,2048]{1,0:T(8,128)S(1)} %fusion.276, f32[1024,1024]{1,0:T(8,128)S(1)} %copy-done.2, f32[2048,1024]{1,0:T(8,128)} %param.8, f32[1024]{0:T(1024)S(1)} %multiply_reduce_fusion.1, f32[2048]{0:T(1024)S(1)} %multiply_reduce_fusion), kind=kOutput, calls=%fused_computation.20 | convolution fusion | flops 12897484800 | bytes 29372416 | tf_op jit(solution)/shard_map/dot_general | solution.py:21
  197.9 9.5 %fusion = f32[256,1280]{0,1:T(8,128)} fusion(f32[2048,256]{0,1:T(8,128)S(1)} %copy-done.18, f32[2048,1024]{0,1:T(8,128)} %bitcast_subtract_fusion), kind=kOutput, calls=%fused_computation.17 | convolution fusion | flops 4029153280 | bytes 13893632 | tf_op jit(solution)/shard_map/dot_general | solution.py:15
  226.1 132.8 %all-reduce.6.cloned.1.call-done = (f32[256,512]{0,1:T(8,128)}, f32[256,1280]{0,1:T(8,128)}, f32[256,1024]{0,1:T(8,128)}, f32[256,768]{0,1:T(8,128)}) async-done(((f32[256,512]{0,1:T(8,128)}, f32[256,1280]{0,1:T(8,128)}, f32[256,1024]{0,1:T(8,128)}, f32[256,768]{0,1:T(8,128)}), (f32[256,512]{0,1:T(8,128)}, f32[256,1280]{0,1:T(8,128)}, f32[256,1024]{0,1:T(8,128)}, ...) | async-done | bytes 3670032 | tf_op jit(solution)/shard_map/psum | solution.py:121
  361.0 11.7 %cholesky.214 = f32[128,128]{1,0:T(8,128)S(1)} custom-call(f32[128,128]{1,0:T(8,128)S(1)} %cholesky.346), custom_call_target="Cholesky" | custom-call | tf_op jit(solution)/shard_map/jit(cholesky)/cholesky | solution.py:69
  372.8 9.8 %custom-call.17 = f32[1,128,128]{1,2,0:T(8,128)S(1)} custom-call(f32[1,128,128]{2,1,0:T(8,128)S(1)} %get-tuple-element.101), custom_call_target="InvertDiagBlocksLowerTriangular" | custom-call | tf_op jit(solution)/shard_map/jit(cholesky)/cholesky | solution.py:69
  383.1 11.9 %cholesky.231 = f32[128,128]{1,0:T(8,128)S(1)} custom-call(f32[128,128]{1,0:T(8,128)S(1)} %convolution_subtract_fusion.28), custom_call_target="Cholesky" | custom-call | tf_op jit(solution)/shard_map/jit(cholesky)/cholesky | solution.py:69
  401.1 19.7 %custom-call.18 = f32[2,128,128]{1,2,0:T(8,128)S(1)} custom-call(f32[2,128,128]{2,1,0:T(8,128)S(1)} %get-tuple-element.30), custom_call_target="InvertDiagBlocksLowerTriangular" | custom-call | tf_op jit(solution)/shard_map/triangular_solve/custom-call.0 | solution.py:71
  440.9 11.7 %cholesky.248 = f32[128,128]{1,0:T(8,128)S(1)} custom-call(f32[128,128]{1,0:T(8,128)S(1)} %cholesky.349), custom_call_target="Cholesky" | custom-call | tf_op jit(solution)/shard_map/jit(cholesky)/cholesky | solution.py:69
  452.6 9.8 %custom-call.19 = f32[1,128,128]{1,2,0:T(8,128)S(1)} custom-call(f32[1,128,128]{2,1,0:T(8,128)S(1)} %get-tuple-element.97), custom_call_target="InvertDiagBlocksLowerTriangular" | custom-call | tf_op jit(solution)/shard_map/jit(cholesky)/cholesky | solution.py:69
  462.9 11.7 %cholesky.265 = f32[128,128]{1,0:T(8,128)S(1)} custom-call(f32[128,128]{1,0:T(8,128)S(1)} %convolution_subtract_fusion.27), custom_call_target="Cholesky" | custom-call | tf_op jit(solution)/shard_map/jit(cholesky)/cholesky | solution.py:69
  481.4 19.9 %custom-call.20 = f32[2,128,128]{1,2,0:T(8,128)S(1)} custom-call(f32[2,128,128]{2,1,0:T(8,128)S(1)} %get-tuple-element.31), custom_call_target="InvertDiagBlocksLowerTriangular" | custom-call | tf_op jit(solution)/shard_map/triangular_solve/custom-call.0 | solution.py:71
  525.8 11.7 %cholesky.282 = f32[128,128]{1,0:T(8,128)S(1)} custom-call(f32[128,128]{1,0:T(8,128)S(1)} %cholesky.352), custom_call_target="Cholesky" | custom-call | tf_op jit(solution)/shard_map/jit(cholesky)/cholesky | solution.py:69
  538.3 9.8 %custom-call.21 = f32[1,128,128]{1,2,0:T(8,128)S(1)} custom-call(f32[1,128,128]{2,1,0:T(8,128)S(1)} %get-tuple-element.93), custom_call_target="InvertDiagBlocksLowerTriangular" | custom-call | tf_op jit(solution)/shard_map/jit(cholesky)/cholesky | solution.py:69
  550.9 11.9 %cholesky.299 = f32[128,128]{1,0:T(8,128)S(1)} custom-call(f32[128,128]{1,0:T(8,128)S(1)} %convolution_subtract_fusion.26), custom_call_target="Cholesky" | custom-call | tf_op jit(solution)/shard_map/jit(cholesky)/cholesky | solution.py:69
  567.7 5.8 while.10
  574.1 20.5 %custom-call.22 = f32[2,128,128]{1,2,0:T(8,128)S(1)} custom-call(f32[2,128,128]{2,1,0:T(8,128)} %copy-done.27), custom_call_target="InvertDiagBlocksLowerTriangular" | custom-call | tf_op jit(solution)/shard_map/triangular_solve/custom-call.0 | solution.py:71
  620.7 11.7 %cholesky.316 = f32[128,128]{1,0:T(8,128)S(1)} custom-call(f32[128,128]{1,0:T(8,128)S(1)} %cholesky.355), custom_call_target="Cholesky" | custom-call | tf_op jit(solution)/shard_map/jit(cholesky)/cholesky | solution.py:69
  632.5 9.8 %custom-call.23 = f32[1,128,128]{1,2,0:T(8,128)S(1)} custom-call(f32[1,128,128]{2,1,0:T(8,128)S(1)} %get-tuple-element.89), custom_call_target="InvertDiagBlocksLowerTriangular" | custom-call | tf_op jit(solution)/shard_map/jit(cholesky)/cholesky | solution.py:69
  644.4 11.9 %cholesky.333 = f32[128,128]{1,0:T(8,128)S(1)} custom-call(f32[128,128]{1,0:T(8,128)S(1)} %convolution_subtract_fusion.25), custom_call_target="Cholesky" | custom-call | tf_op jit(solution)/shard_map/jit(cholesky)/cholesky | solution.py:69
  663.9 20.3 %custom-call.24 = f32[2,128,128]{1,2,0:T(8,128)} custom-call(f32[2,128,128]{2,1,0:T(8,128)S(1)} %get-tuple-element.33), custom_call_target="InvertDiagBlocksLowerTriangular" | custom-call | tf_op jit(solution)/shard_map/triangular_solve/custom-call.0 | solution.py:71
  699.7 11.7 %convolution_subtract_fusion = f32[2048,256]{1,0:T(8,128)} fusion(f32[2048,256]{1,0:T(8,128)S(1)} %copy-done.5, f32[2048,1024]{0,1:T(8,128)} %bitcast_subtract_fusion, f32[256,256]{1,0:T(8,128)S(1)} %fusion.145, f32[256,256]{1,0:T(8,128)S(1)} %convolution_subtract_fusion.17, f32[256,256]{1,0:T(8,128)S(1)} %convolution_subtract_fusion.20, ...), kind=kOutput, calls=%fused_computation.32 | convolution fusion | flops 3222536192 | bytes 13631488 | tf_op jit(solution)/shard_map/dot_general | solution.py:11
  (257 shorter events, 164.7 us)
Async XLA Ops:
  7.2 167.4 %all-reduce.8.cloned.1.call-start = ((), (), s32[]{:S(2)}) async-start(), calls=%async_computation.1 | async-start | bytes 9437184 | tf_op jit(solution)/shard_map/psum | solution.py:116
  8.7 9.9 %copy-start = (f32[2048,128]{1,0:T(8,128)S(1)}, f32[2048,128]{1,0:T(8,128)}, u32[]{:S(2)}) copy-start(f32[2048,128]{1,0:T(8,128)} %param.7) | copy-start | bytes 3145732
  27.1 331.8 %all-reduce.6.cloned.1.call-start = ((), (), s32[]{:S(2)}) async-start(), calls=%async_computation | async-start | bytes 7340032 | tf_op jit(solution)/shard_map/psum | solution.py:121
  30.0 564.9 %copy-start.9 = (f32[256,256]{0,1:T(8,128)}, f32[256,256]{0,1:T(8,128)S(1)}, u32[]{:S(2)}) copy-start(f32[256,256]{0,1:T(8,128)S(1)} %fusion.132) | copy-start | bytes 786436
  174.5 4.7 copy-start.1
  174.5 4.9 copy-start.2
  179.5 18.5 %copy-start.18 = (f32[2048,256]{0,1:T(8,128)S(1)}, f32[2048,256]{0,1:T(8,128)}, u32[]{:S(2)}) copy-start(f32[2048,256]{0,1:T(8,128)} %copy.6) | copy-start | bytes 6291460
  197.9 9.6 %copy-start.4 = (f32[2048,1024]{0,1:T(8,128)S(1)}, f32[2048,1024]{0,1:T(8,128)}, u32[]{:S(2)}) copy-start(f32[2048,1024]{0,1:T(8,128)} %bitcast_subtract_fusion) | copy-start | bytes 25165828
  218.8 5.8 copy-start.3
  226.0 203.9 %copy-start.6 = (f32[768,256]{1,0:T(8,128)}, f32[768,256]{1,0:T(8,128)S(1)}, u32[]{:S(2)}) copy-start(f32[768,256]{1,0:T(8,128)S(1)} %fusion.21) | copy-start | bytes 2359300
  427.5 7.0 copy-start.22
  503.7 11.6 %copy-start.17 = (f32[256,256]{0,1:T(8,128)}, f32[256,256]{0,1:T(8,128)S(1)}, u32[]{:S(2)}) copy-start(f32[256,256]{0,1:T(8,128)S(1)} %fusion.107) | copy-start | bytes 786436
  507.3 7.1 copy-start.15
  507.3 4.7 copy-start.25
  511.6 4.9 copy-start.8
  518.0 1.8 copy-start.11
  594.6 7.7 %copy-start.16 = (f32[512,256]{1,0:T(8,128)S(1)}, f32[512,256]{1,0:T(8,128)}, u32[]{:S(2)}) copy-start(f32[512,256]{1,0:T(8,128)} %copy-done.15) | copy-start | bytes 1572868
  603.9 6.0 copy-start.14
  604.6 6.4 copy-start.26
  608.8 7.0 copy-start.12
  616.5 67.8 %copy-start.10 = (f32[256,256]{0,1:T(8,128)S(1)}, f32[256,256]{0,1:T(8,128)}, u32[]{:S(2)}) copy-start(f32[256,256]{0,1:T(8,128)} %copy-done.9) | copy-start | bytes 786436
  656.3 2.6 copy-start.21
  692.8 4.5 copy-start.20
  694.8 4.9 copy-start.5
  (6 other events, 4.6 us)
Sparse Core Ops, SparseCore 0:
  27.2 147.3 all-reduce.7
  218.9 139.8 all-reduce.5

commit v2 on v1

--- a/solution.py
+++ b/solution.py
@@ -1,10 +1,14 @@
 import jax
 import jax.numpy as jnp
 from jax import lax
+from jax.experimental import pallas as pl
+from jax.experimental.pallas import tpu as pltpu
 from jax.sharding import PartitionSpec as P
 
 LOAD = 0.05
 RIDGE = 0.1
+PANEL = 64
+GROUP = 4
 
 
 def dot(a, b, precision=lax.Precision.HIGH):
@@ -65,10 +69,50 @@
     return est
 
 
+def panel_inverse(mat):
+    n = mat.shape[0]
+    row_id = lax.broadcasted_iota(jnp.int32, (n, 2 * n), 0)
+    lane_id = lax.broadcasted_iota(jnp.int32, (n, 2 * n), 1)
+    eye = (row_id == lane_id - n).astype(jnp.float32)
+    work = jnp.concatenate([mat, eye[:, n:]], axis=1)
+    for start in range(0, n, GROUP):
+        heads = [
+            jnp.broadcast_to(work[:, start + q : start + q + 1], (n, 2 * n)) for q in range(GROUP)
+        ]
+        for q in range(GROUP):
+            k = start + q
+            mult = jnp.where(row_id > k, heads[q] * (1.0 / heads[q][k : k + 1, :]), 0.0)
+            for p in range(q + 1, GROUP):
+                heads[p] = heads[p] - mult * heads[p][k : k + 1, :]
+            work = work - mult * work[k : k + 1, :]
+    diag = jnp.sum(jnp.where(row_id == lane_id, work, 0.0), axis=1, keepdims=True)
+    return work[:, n:] * (1.0 / jnp.sqrt(diag))
+
+
+def inverse_lower(mat):
+    n = mat.shape[0]
+    if n <= PANEL:
+        return panel_inverse(mat)
+    h = n // 2
+    top = inverse_lower(mat[:h, :h])
+    side = fdot_nt(mat[h:, :h], top)
+    bottom = inverse_lower(mat[h:, h:] - fdot_nt(side, side))
+    corner = -fdot(bottom, fdot(side, top))
+    upper = jnp.concatenate([top, jnp.zeros((h, h), jnp.float32)], axis=1)
+    return jnp.concatenate([upper, jnp.concatenate([corner, bottom], axis=1)], axis=0)
+
+
+def factor_kernel(mat_ref, out_ref):
+    out_ref[...] = inverse_lower(mat_ref[...])
+
+
 def factor_inverse(mat):
-    lower = jnp.linalg.cholesky(mat)
-    eye = jnp.eye(mat.shape[0], dtype=jnp.float32)
-    return lax.linalg.triangular_solve(lower, eye, left_side=True, lower=True)
+    return pl.pallas_call(
+        factor_kernel,
+        out_shape=jax.ShapeDtypeStruct(mat.shape, jnp.float32),
+        in_specs=[pl.BlockSpec(memory_space=pltpu.VMEM)],
+        out_specs=pl.BlockSpec(memory_space=pltpu.VMEM),
+    )(mat)
 
 
 def chain(grams, at_pivots, blocks, piv, npts):

time: 727 us -> 515 us (0.71)
  other arithmetic: 241 us -> 15.1 us
  Pallas kernels: 0 us -> 61.7 us
  local copies, waits for them, and re-layouts: 43.9 us -> 19.1 us
  matrix products: 135 us -> 119 us
    another operation x36 -> x0, other arithmetic: 222 us -> none  [the longest x27 139 us: factor_inverse(): lower = jnp.linalg.cholesky(mat)]
    pallas_call x0 -> x4, Pallas kernels: none -> 61.7 us  [factor_inverse(): pl.pallas_call(factor_kernel, out_shape=jax.ShapeDtypeStruct(mat.shape, j...]
    another operation x37 -> x0, local copies, waits for them, and re-layouts: 18.5 us -> none  [the longest x29 17.7 us: factor_inverse(): return lax.linalg.triangular_solve(lower, eye, left_side=True, lower=True)]
    another operation x20 -> x0, matrix products: 12.4 us -> none  [the longest x12 6.56 us: factor_inverse(): return lax.linalg.triangular_solve(lower, eye, left_side=True, lower=True)]
  transfers between devices with their start and end apart: 2 -> 2, of which waited for: 2 -> 2; matrix products, arithmetic and copies ran while one was open for 1% -> 2% of each run, Pallas kernels for 0% -> 0%
where the time goes in v2:
time: 515 us; the launch traced here: 507 us
  waiting for transfers between devices  277 us (54%)
  matrix products  119 us (23%)
  Pallas kernels  61.7 us (12%)
  local copies, waits for them, and re-layouts  19.1 us (4%)
  between operations  15.5 us (3%)
  other arithmetic  15.1 us (3%)
    psum x1, waiting for transfers between devices, per_device(): lax.psum((owned_rows(features, idx, offset, count), owned_rows(factor, id...  144 us
    psum x1, waiting for transfers between devices, per_device(): lax.psum([dot_tn(cols[:, c * piv:(c + 1) * piv], joined[:, c * piv:]) for...  133 us
    pallas_call x4, Pallas kernels, factor_inverse(): pl.pallas_call(factor_kernel, out_shape=jax.ShapeDtypeStruct(mat.shape, j...  61.7 us
    dot_general x50, matrix products, dot(): jnp.dot(a, b, precision=precision, preferred_element_type=jnp.float32)  40.8 us
    dot_general x20, matrix products, dot_tn(): lax.dot_general(a, b, (((0,), (0,)), ((), ())), precision=precision, pref...  39.8 us
    dot_general x15, matrix products, dot_nt(): lax.dot_general(a, b, (((1,), (1,)), ((), ())), precision=precision, pref...  38.9 us
    gather x2, local copies, waits for them, and re-layouts, owned_rows(): return jnp.take(table, safe, axis=0) * owned[:, None].astype(table.dtype)  13.8 us
  transfers between devices with their start and end apart: 2, of which 2 were waited for; matrix products, arithmetic and copies ran while one was open for 2% of the time, Pallas kernels for 0%

profile of v2, /device:TPU:0, one launch (start us, length us, event | category | flops | bytes accessed | tf_op | source)
XLA Modules:
  0.0 507.4 jit_solution(11170802463261102586)
XLA Ops:
  8.7 4.0 gather_fusion
  12.7 9.8 %gather_fusion.1 = f32[1024,1024]{1,0:T(8,128)} fusion(f32[2048,1024]{1,0:T(8,128)} %param.5, s32[1024]{0:T(1024)S(1)} %broadcast_clamp_fusion), kind=kCustom, calls=%fused_computation.1 | custom fusion | bytes 8392704 | tf_op jit(solution)/shard_map/jit(_take)/gather | solution.py:54
  23.6 4.6 select_multiply_fusion
  29.7 1.8 copy.6
  31.9 143.9 %all-reduce.7.cloned.1.call-done = (f32[1024,128]{1,0:T(8,128)}, f32[1024,1024]{1,0:T(8,128)}) async-done(((f32[1024,128]{1,0:T(8,128)}, f32[1024,1024]{1,0:T(8,128)}), (f32[1024,128]{1,0:T(8,128)}, f32[1024,1024]{1,0:T(8,128)})) %all-reduce.7.cloned.1.call-update) | async-done | bytes 4718608 | tf_op jit(solution)/shard_map/psum | solution.py:160
  177.1 4.7 fusion.226
  181.8 18.7 %bitcast_subtract_fusion = f32[2048,1024]{0,1:T(8,128)} fusion(f32[1024,2048]{1,0:T(8,128)S(1)} %fusion.226, f32[1024,1024]{1,0:T(8,128)S(1)} %copy-done.2, f32[2048,1024]{1,0:T(8,128)} %param.5, f32[1024]{0:T(1024)S(1)} %multiply_reduce_fusion.1, f32[2048]{0:T(1024)S(1)} %multiply_reduce_fusion), kind=kOutput, calls=%fused_computation.12 | convolution fusion | flops 12897484800 | bytes 29372416 | tf_op jit(solution)/shard_map/dot_general | solution.py:25
  200.5 5.0 fusion.11
  205.6 6.7 %fusion.8 = f32[256,768]{1,0:T(8,128)} fusion(f32[2048,1024]{0,1:T(8,128)} %bitcast_subtract_fusion, f32[2048,256]{0,1:T(8,128)S(1)} %copy-done.22), kind=kOutput, calls=%fused_computation.18 | convolution fusion | flops 2417491968 | bytes 13369344 | tf_op jit(solution)/shard_map/dot_general | solution.py:19
  212.3 4.9 fusion.2
  217.2 6.1 %fusion = f32[256,1280]{1,0:T(8,128)} fusion(f32[2048,256]{0,1:T(8,128)S(1)} %copy-done.22, f32[2048,1024]{0,1:T(8,128)S(1)} %bitcast.131), kind=kOutput, calls=%fused_computation.9 | convolution fusion | flops 4029153280 | bytes 13893632 | tf_op jit(solution)/shard_map/dot_general | solution.py:19
  224.0 2.4 fusion.47
  230.7 132.6 %all-reduce.5.cloned.1.call-done = (f32[256,512]{1,0:T(8,128)}, f32[256,1280]{1,0:T(8,128)}, f32[256,1024]{1,0:T(8,128)}, f32[256,768]{1,0:T(8,128)}) async-done(((f32[256,512]{1,0:T(8,128)}, f32[256,1280]{1,0:T(8,128)}, f32[256,1024]{1,0:T(8,128)}, f32[256,768]{1,0:T(8,128)}), (f32[256,512]{1,0:T(8,128)}, f32[256,1280]{1,0:T(8,128)}, f32[256,1024]{1,0:T(8,128)}, ...) | async-done | bytes 3670032 | tf_op jit(solution)/shard_map/psum | solution.py:165
  363.3 1.7 select_add_fusion.3.mat_ref
  365.0 15.3 %shard_map.59 = f32[256,256]{1,0:T(8,128)} custom-call(f32[256,256]{1,0:T(8,128)} %select_add_fusion.3.mat_ref), custom_call_target="tpu_custom_call" | custom-call | tf_op jit(solution)/shard_map/pallas_call | solution.py:110
  390.3 2.3 convolution_subtract_fusion.2
  392.7 2.0 convolution_subtract_fusion.3
  397.4 15.7 %shard_map.60 = f32[256,256]{1,0:T(8,128)} custom-call(f32[256,256]{1,0:T(8,128)} %select_add_fusion.2.mat_ref), custom_call_target="tpu_custom_call" | custom-call | tf_op jit(solution)/shard_map/pallas_call | solution.py:110
  416.0 2.1 convolution_subtract_fusion.8
  430.5 15.3 %shard_map.61 = f32[256,256]{1,0:T(8,128)} custom-call(f32[256,256]{1,0:T(8,128)} %select_add_fusion.1.mat_ref), custom_call_target="tpu_custom_call" | custom-call | tf_op jit(solution)/shard_map/pallas_call | solution.py:110
  450.3 1.8 convolution_subtract_fusion.15
  453.2 1.6 convolution_subtract_fusion.13
  463.0 15.4 %shard_map.62 = f32[256,256]{1,0:T(8,128)} custom-call(f32[256,256]{1,0:T(8,128)} %select_add_fusion.mat_ref), custom_call_target="tpu_custom_call" | custom-call | tf_op jit(solution)/shard_map/pallas_call | solution.py:110
  487.5 11.6 %convolution_subtract_fusion = f32[2048,256]{1,0:T(8,128)} fusion(f32[2048,256]{1,0:T(8,128)S(1)} %copy-done.9, f32[2048,1024]{0,1:T(8,128)} %bitcast_subtract_fusion, f32[256,256]{1,0:T(8,128)S(1)} %fusion.231, f32[256,256]{1,0:T(8,128)S(1)} %convolution_subtract_fusion.17, f32[256,256]{1,0:T(8,128)S(1)} %convolution_subtract_fusion.20, ...), kind=kOutput, calls=%fused_computation.24 | convolution fusion | flops 3222536192 | bytes 13631488 | tf_op jit(solution)/shard_map/dot_general | solution.py:15
  (153 shorter events, 61.8 us)
Async XLA Ops:
  7.2 168.6 %all-reduce.7.cloned.1.call-start = ((), (), s32[]{:S(2)}) async-start(), calls=%async_computation.1 | async-start | bytes 9437184 | tf_op jit(solution)/shard_map/psum | solution.py:160
  28.1 3.4 copy-start
  28.2 335.1 %all-reduce.5.cloned.1.call-start = ((), (), s32[]{:S(2)}) async-start(), calls=%async_computation | async-start | bytes 7340032 | tf_op jit(solution)/shard_map/psum | solution.py:165
  177.0 4.7 copy-start.2
  181.8 18.8 %copy-start.22 = (f32[2048,256]{0,1:T(8,128)S(1)}, f32[2048,256]{0,1:T(8,128)}, u32[]{:S(2)}) copy-start(f32[2048,256]{0,1:T(8,128)} %copy.6) | copy-start | bytes 6291460
  200.5 11.8 %slice-start = ((s8[8388608]{0:T(1024)(128)(4,1)}), s8[4194304]{0:T(1024)(128)(4,1)S(1)}, s32[]{:S(2)}) async-start(s8[8388608]{0:T(1024)(128)(4,1)} %bitcast.130), calls=%async_computation.2 | async-start | bytes 8388608
  205.6 6.7 %slice-start.1 = ((s8[8388608]{0:T(1024)(128)(4,1)}), s8[4194304]{0:T(1024)(128)(4,1)S(1)}, s32[]{:S(2)}) async-start(s8[8388608]{0:T(1024)(128)(4,1)} %bitcast.130), calls=%async_computation.3 | async-start | bytes 8388608
  217.2 6.2 %copy-start.1 = (f32[1024,128]{1,0:T(8,128)S(1)}, f32[1024,128]{1,0:T(8,128)}, u32[]{:S(2)}) copy-start(f32[1024,128]{1,0:T(8,128)} %get-tuple-element.10) | copy-start | bytes 1572868
  223.4 5.8 %copy-start.3 = (f32[1024,1024]{1,0:T(8,128)S(1)}, f32[1024,1024]{1,0:T(8,128)}, u32[]{:S(2)}) copy-start(f32[1024,1024]{1,0:T(8,128)} %get-tuple-element.11) | copy-start | bytes 12582916
  230.7 158.2 %copy-start.10 = (f32[768,256]{1,0:T(8,128)}, f32[768,256]{1,0:T(8,128)S(1)}, u32[]{:S(2)}) copy-start(f32[768,256]{1,0:T(8,128)S(1)} %fusion.21) | copy-start | bytes 2359300
  380.3 6.3 %copy-start.7 = (f32[256,256]{1,0:T(8,128)S(1)}, f32[256,256]{1,0:T(8,128)}, u32[]{:S(2)}) copy-start(f32[256,256]{1,0:T(8,128)} %shard_map.59) | copy-start | bytes 786436
  386.7 6.0 %copy-start.23 = (f32[256,1024]{1,0:T(8,128)S(1)}, f32[256,1024]{1,0:T(8,128)}, u32[]{:S(2)}) copy-start(f32[256,1024]{1,0:T(8,128)} %get-tuple-element.8) | copy-start | bytes 3145732
  419.0 4.5 copy-start.4
  419.0 4.5 copy-start.20
  419.0 4.5 copy-start.21
  447.3 7.5 %copy-start.13 = (f32[256,768]{1,0:T(8,128)S(1)}, f32[256,768]{1,0:T(8,128)}, u32[]{:S(2)}) copy-start(f32[256,768]{1,0:T(8,128)} %copy-done.12) | copy-start | bytes 2359300
  448.8 10.4 %copy-start.18 = (f32[256,256]{1,0:T(8,128)}, f32[256,256]{1,0:T(8,128)S(1)}, u32[]{:S(2)}) copy-start(f32[256,256]{1,0:T(8,128)S(1)} %fusion.101) | copy-start | bytes 786436
  450.3 5.1 %copy-start.5 = (f32[256,256]{1,0:T(8,128)S(1)}, f32[256,256]{1,0:T(8,128)}, u32[]{:S(2)}) copy-start(f32[256,256]{1,0:T(8,128)} %shard_map.61) | copy-start | bytes 786436
  455.8 4.4 copy-start.17
  463.0 21.6 %copy-start.19 = (f32[256,256]{1,0:T(8,128)S(1)}, f32[256,256]{1,0:T(8,128)}, u32[]{:S(2)}) copy-start(f32[256,256]{1,0:T(8,128)} %copy-done.18) | copy-start | bytes 786436
  481.1 3.9 copy-start.11
  483.8 3.7 copy-start.9
  487.5 11.7 %copy-start.24 = (f32[1,256,256]{2,1,0:T(8,128)S(1)}, f32[1,256,256]{2,1,0:T(8,128)}, u32[]{:S(2)}) copy-start(f32[1,256,256]{2,1,0:T(8,128)} %get-tuple-element.16) | copy-start | bytes 786436
  487.5 11.7 %copy-start.25 = (f32[1,256,256]{2,1,0:T(8,128)S(1)}, f32[1,256,256]{2,1,0:T(8,128)}, u32[]{:S(2)}) copy-start(f32[1,256,256]{2,1,0:T(8,128)} %get-tuple-element.17) | copy-start | bytes 786436
  (6 other events, 10.5 us)
Sparse Core Ops, SparseCore 0:
  28.3 147.4 all-reduce.6
  223.5 139.7 all-reduce.4
